TPU v7x, 32 devices: a whole 2x2x4 slice. The times are simulated.
32 devices in a mesh: tgt: 16 (over z, y, core), sup: 2 (over x).
Axes of the slice: x: 2, y: 2, z: 4, core: 2. Of those that a mesh axis runs over, the one named last changes fastest.
Arguments:
- targets: bfloat16 [3584, 12288], P('tgt', 'sup'), may hold values from -6 to 6, as said below
- support: bfloat16 [128, 12288], P('sup'), may hold values from -6 to 6, as said below
- label_weights: bfloat16 [128, 1000], P('sup'), may hold values from -0.00390625 to 0.00390625
- labels: int32 [3584], P('tgt'), may hold values from 0 to 999
- first_moment: float32 [128, 12288], P('sup', 'tgt'), may hold values from -0.6 to 0.6
- second_moment: float32 [128, 12288], P('sup', 'tgt'), may hold values from 0.001 to 0.1
Outputs:
- new_support: bfloat16 [128, 12288], P('sup')
- new_first: float32 [128, 12288], P('sup', 'tgt')
- new_second: float32 [128, 12288], P('sup', 'tgt')
Inputs may be any that keep to these rules, and one draw needn't show every extreme that they name: `targets`: image pixel values. `support`: image pixel values.
All inputs are finite; a program needn't handle non-finite values.
Results may differ from a plain program's by a relative error of at most 0.0028.
Values may be sent and summed in bfloat16 or wider, within the bound.
A program may use at most 64 MiB of HBM per device.

v0:
```python
import math

import jax
import jax.numpy as jnp
from jax import lax
from jax.sharding import PartitionSpec as P

DEPTH = 3


bias_var = 0.1
learning_rate = 0.05
first_decay = 0.9
second_decay = 0.99
first_fix = 1.0 - 0.9**10
second_fix = 1.0 - 0.99**10
adam_eps = 1e-08


def tangent_kernel(cross, target_diag, support_diag):
    tangent = cross
    current = cross
    left_diag = target_diag
    right_diag = support_diag
    for _ in range(DEPTH):
        product = (1.0 + 2.0 * left_diag)[:, None] * (1.0 + 2.0 * right_diag)[None, :]
        slope = 4.0 / math.pi / jnp.sqrt(product - 4.0 * current * current)
        current = 2.0 / math.pi * jnp.arcsin(2.0 * current / jnp.sqrt(product)) + bias_var
        tangent = current + slope * tangent
        left_diag = 2.0 / math.pi * jnp.arcsin(2.0 * left_diag / (1.0 + 2.0 * left_diag)) + bias_var
        right_diag = (
            2.0 / math.pi * jnp.arcsin(2.0 * right_diag / (1.0 + 2.0 * right_diag)) + bias_var
        )
    return tangent


def row_squares(images):
    return jnp.sum(jnp.square(images.astype(jnp.float32)), axis=1)


def shards(targets, support, label_weights, labels, first_moment, second_moment):
    pixels = support.shape[1]
    target_count = targets.shape[0] * lax.axis_size("tgt")
    support_count = support.shape[0] * lax.axis_size("sup")
    class_count = label_weights.shape[1]
    support_diag = row_squares(support) / pixels + bias_var
    slabs = lax.all_to_all(support, "sup", split_axis=1, concat_axis=0, tiled=True)
    partial_cross = lax.dot_general(
        targets, slabs, (((1,), (1,)), ((), ())), preferred_element_type=jnp.float32
    )
    cross = (
        lax.psum_scatter(
            partial_cross.astype(jnp.bfloat16), "sup", scatter_dimension=1, tiled=True
        ).astype(jnp.float32)
        / pixels
        + bias_var
    )
    target_diag = lax.psum(row_squares(targets), "sup") / pixels + bias_var

    def kernel_of(cross_in, diag_in):
        return tangent_kernel(cross_in, target_diag, diag_in)

    kernel, pullback = jax.vjp(kernel_of, cross, support_diag)
    partial_pred = jnp.dot(
        kernel.astype(jnp.bfloat16), label_weights, preferred_element_type=jnp.float32
    )
    predicted = lax.psum(partial_pred.astype(jnp.bfloat16), "sup").astype(jnp.float32)
    classes = jnp.arange(class_count, dtype=jnp.int32)
    onehot = (labels[:, None] == classes[None, :]).astype(jnp.float32)
    residual = (predicted - onehot).astype(jnp.bfloat16)
    kernel_grad = lax.dot_general(
        residual, label_weights, (((1,), (1,)), ((), ())), preferred_element_type=jnp.float32
    )
    kernel_grad = kernel_grad * (
        4.0 * pixels * math.sqrt(class_count * support_count / target_count)
    )
    cross_grad, norm_grad = pullback(kernel_grad)
    cross_low = cross_grad.astype(jnp.bfloat16)
    all_grads = lax.all_gather(cross_low, "sup", axis=1, tiled=True)
    slab_grad = lax.dot_general(
        all_grads, targets, (((0,), (0,)), ((), ())), preferred_element_type=jnp.float32
    )
    image_grad = lax.all_to_all(
        slab_grad.astype(jnp.bfloat16), "sup", split_axis=0, concat_axis=1, tiled=True
    ).astype(slab_grad.dtype)
    gradient = (image_grad + 2.0 * norm_grad[:, None] * support.astype(jnp.float32)) / pixels
    shares = lax.psum_scatter(gradient, "tgt", scatter_dimension=1, tiled=True)
    slab_width = shares.shape[1]
    own_pixels = lax.dynamic_slice_in_dim(
        support, lax.axis_index("tgt") * slab_width, slab_width, 1
    ).astype(jnp.float32)
    new_first = first_decay * first_moment + (1.0 - first_decay) * shares
    new_second = second_decay * second_moment + (1.0 - second_decay) * shares * shares
    update = (
        learning_rate * (new_first / first_fix) / (jnp.sqrt(new_second / second_fix) + adam_eps)
    )
    new_slab = (own_pixels - update).astype(jnp.bfloat16)
    new_support = lax.all_gather(new_slab, "tgt", axis=1, tiled=True)
    return (new_support, new_first, new_second)


def solution(mesh):
    return jax.shard_map(
        shards,
        mesh=mesh,
        in_specs=(
            P("tgt", "sup"),
            P("sup", None),
            P("sup", None),
            P("tgt"),
            P("sup", "tgt"),
            P("sup", "tgt"),
        ),
        out_specs=(P("sup", None), P("sup", "tgt"), P("sup", "tgt")),
        check_vma=False,
    )
```

profile of v0, /device:TPU:1, one launch (start us, length us, event | category | flops | bytes accessed | tf_op | source)
XLA Modules:
  0.0 233.3 jit_solution(4970678291514561601)
XLA Ops:
  7.2 0.0 copy-start
  7.2 0.0 copy-start.1
  7.2 2.8 %copy.18 = bf16[8,2,8,6144]{3,2,0,1:T(8,128)(2,1)} copy(bf16[8,2,8,6144]{3,2,1,0:T(8,128)(2,1)} %bitcast.18) | data formatting | bytes 3145728 | tf_op jit(solution)/shard_map/all_to_all | solution.py:47
  10.0 4.6 %all-to-all-start = ((bf16[64,2,6144]{2,0,1:T(8,128)(2,1)}), bf16[64,2,6144]{2,0,1:T(8,128)(2,1)}, u32[]{:S(2)}, u32[]{:S(2)}) async-start(bf16[64,2,6144]{2,0,1:T(8,128)(2,1)} %bitcast.20), calls=%async_computation | async-start | bytes 3145728 | tf_op jit(solution)/shard_map/all_to_all | solution.py:47
  14.6 0.0 reduce-scatter.3.cloned.1.call-start
  14.7 0.0 copy-done.1
  14.7 0.6 multiply_reduce_fusion
  15.3 19.0 %psum.14 = f32[224]{0:T(256)S(1)} all-reduce(f32[224]{0:T(256)S(1)} %multiply_reduce_fusion), channel_id=1, replica_groups=mesh['tgt'=16,'sup'=2] {'sup'}, use_global_device_ids=true, to_apply=%region_1.0 | all-reduce | flops 224 | bytes 1792 | tf_op jit(solution)/shard_map/psum | solution.py:58
  34.3 1.8 fusion
  36.1 0.1 broadcast_add_fusion
  36.2 0.1 multiply_add_fusion.6
  36.3 0.1 broadcast_add_fusion.2
  36.3 0.0 all-to-all-done
  36.4 0.0 copy-start.6
  36.4 3.1 %convolution_convert_fusion.2 = bf16[224,128]{0,1:T(8,128)(2,1)} fusion(bf16[224,6144]{1,0:T(8,128)(2,1)S(1)} %copy-done.1, bf16[128,6144]{1,0:T(8,128)(2,1)} %bitcast.1), kind=kOutput, calls=%fused_computation.10 | convolution fusion | flops 352350208 | bytes 4382720 | tf_op jit(solution)/shard_map/dot_general | solution.py:48
  39.5 0.0 reduce-scatter.3.cloned.1.call-update
  39.5 0.0 all-reduce.2.cloned.1.call-start
  39.6 0.1 multiply_add_fusion.7
  39.6 10.6 %reduce-scatter.3.cloned.1.call-done = bf16[224,64]{0,1:T(8,128)(2,1)} async-done(((bf16[224,128]{0,1:T(8,128)(2,1)}), bf16[224,64]{0,1:T(8,128)(2,1)}) %reduce-scatter.3.cloned.1.call-update) | async-done | bytes 28688 | tf_op jit(solution)/shard_map/reduce_scatter | solution.py:52
  50.2 0.0 copy-start.5
  50.2 0.0 copy-done
  50.2 2.6 %convolution_convert_fusion.1 = bf16[224,1000]{1,0:T(8,128)(2,1)} fusion(bf16[64,1000]{1,0:T(8,128)(2,1)S(1)} %copy-done, f32[64]{0:T(128)S(1)} %multiply_add_fusion.7, f32[224]{0:T(256)S(1)} %multiply_add_fusion.6, f32[64]{0:T(128)S(1)} %get-tuple-element.13, f32[224]{0:T(256)S(1)} %get-tuple-element.11, ...), kind=kOutput, calls=%fused_computation.9 | convolution fusion | flops 29641472 | bytes 608128 | tf_op jit(solution)/shard_map/dot_general | solution.py:64
  52.8 0.0 all-reduce.2.cloned.1.call-update
  52.8 27.9 %all-reduce.2.cloned.1.call-done = bf16[224,1000]{1,0:T(8,128)(2,1)} async-done(((bf16[224,1000]{1,0:T(8,128)(2,1)}), bf16[224,1000]{1,0:T(8,128)(2,1)}) %all-reduce.2.cloned.1.call-update) | async-done | bytes 448016 | tf_op jit(solution)/shard_map/psum | solution.py:67
  80.8 0.0 copy-done.6
  80.8 0.0 copy-done.5
  80.8 1.8 fusion.52
  82.5 0.8 fusion.63
  83.3 0.2 fusion.60
  83.5 3.4 %all_gather.6 = bf16[224,128]{0,1:T(8,128)(2,1)S(1)} all-gather(bf16[224,64]{0,1:T(8,128)(2,1)S(1)} %fusion.60), channel_id=1, replica_groups=mesh['tgt'=16,'sup'=2] {'sup'}, dimensions={1}, use_global_device_ids=true | all-gather | bytes 86016 | tf_op jit(solution)/shard_map/all_gather | solution.py:79
  86.9 1.7 convolution_convert_fusion
  88.7 3.7 %all-to-all-start.1 = ((bf16[2,64,6144]{2,1,0:T(8,128)(2,1)}), bf16[2,64,6144]{2,1,0:T(8,128)(2,1)S(1)}, u32[]{:S(2)}, u32[]{:S(2)}) async-start(bf16[2,64,6144]{2,1,0:T(8,128)(2,1)} %bitcast.21), calls=%async_computation.2 | async-start | bytes 3145728 | tf_op jit(solution)/shard_map/all_to_all | solution.py:83
  92.3 0.0 reduce-scatter.5.cloned.1.call-start
  92.4 17.2 %all-to-all-done.1 = bf16[2,64,6144]{2,1,0:T(8,128)(2,1)S(1)} async-done(((bf16[2,64,6144]{2,1,0:T(8,128)(2,1)}), bf16[2,64,6144]{2,1,0:T(8,128)(2,1)S(1)}, u32[]{:S(2)}, u32[]{:S(2)}) %all-to-all-start.1) | async-done | bytes 1572896 | tf_op jit(solution)/shard_map/all_to_all | solution.py:83
  109.6 0.3 convert_bitcast_fusion
  109.9 0.0 copy-start.2
  110.0 0.2 copy.16
  110.2 1.2 copy-done.2
  111.4 2.2 fusion.2
  113.5 0.0 copy-start.3
  113.5 0.0 copy-start.4
  113.5 0.0 reduce-scatter.5.cloned.1.call-update
  113.6 0.0 all-gather.2.cloned.1.call-start
  113.6 66.7 %reduce-scatter.5.cloned.1.call-done = f32[64,768]{1,0:T(8,128)} async-done(((f32[64,12288]{1,0:T(8,128)}), f32[64,768]{1,0:T(8,128)}) %reduce-scatter.5.cloned.1.call-update) | async-done | bytes 196624 | tf_op jit(solution)/shard_map/reduce_scatter | solution.py:87
  180.3 0.0 copy-done.3
  180.3 0.0 copy-done.4
  180.3 1.8 subtract_convert_fusion.2
  182.1 0.0 all-gather.2.cloned.1.call-update
  182.1 42.0 %all-gather.2.cloned.1.call-done = bf16[64,12288]{1,0:T(8,128)(2,1)} async-done(((bf16[64,768]{1,0:T(8,128)(2,1)}), bf16[64,12288]{1,0:T(8,128)(2,1)}) %all-gather.2.cloned.1.call-update) | async-done | bytes 1572880 | tf_op jit(solution)/shard_map/all_gather | solution.py:98
  224.1 2.7 %copy.21 = bf16[64,12288]{1,0:T(8,128)(2,1)} copy(bf16[64,12288]{1,0:T(8,128)(2,1)} %all-gather.2.cloned.1.call-done) | data formatting | bytes 3145728
  (1 shorter events, 0.0 us)
Async XLA Ops:
  7.2 43.1 %copy-start = (bf16[64,1000]{1,0:T(8,128)(2,1)S(1)}, bf16[64,1000]{1,0:T(8,128)(2,1)}, u32[]{:S(2)}) copy-start(bf16[64,1000]{1,0:T(8,128)(2,1)} %param.8) | copy-start | bytes 384004
  7.2 7.5 %copy-start.1 = (bf16[224,6144]{1,0:T(8,128)(2,1)S(1)}, bf16[224,6144]{1,0:T(8,128)(2,1)}, u32[]{:S(2)}) copy-start(bf16[224,6144]{1,0:T(8,128)(2,1)} %param.6) | copy-start | bytes 8257540
  10.0 26.3 %all-to-all-start = ((bf16[64,2,6144]{2,0,1:T(8,128)(2,1)}), bf16[64,2,6144]{2,0,1:T(8,128)(2,1)}, u32[]{:S(2)}, u32[]{:S(2)}) async-start(bf16[64,2,6144]{2,0,1:T(8,128)(2,1)} %bitcast.20), calls=%async_computation | async-start | bytes 3145728 | tf_op jit(solution)/shard_map/all_to_all | solution.py:47
  14.6 35.6 %reduce-scatter.3.cloned.1.call-start = ((), (), s32[]{:S(2)}) async-start(), calls=%async_computation.4 | async-start | bytes 98304 | tf_op jit(solution)/shard_map/reduce_scatter | solution.py:52
  36.4 44.4 %copy-start.6 = (s32[224]{0:T(256)S(1)}, s32[224]{0:T(256)}, u32[]{:S(2)}) copy-start(s32[224]{0:T(256)} %param.9) | copy-start | bytes 2692
  39.5 41.2 %all-reduce.2.cloned.1.call-start = ((), (), s32[]{:S(2)}) async-start(), calls=%async_computation.5 | async-start | bytes 917504 | tf_op jit(solution)/shard_map/psum | solution.py:67
  50.2 30.5 %copy-start.5 = (bf16[224,64]{0,1:T(8,128)(2,1)S(1)}, bf16[224,64]{0,1:T(8,128)(2,1)}, u32[]{:S(2)}) copy-start(bf16[224,64]{0,1:T(8,128)(2,1)} %reduce-scatter.3.cloned.1.call-done) | copy-start | bytes 86020
  88.7 21.0 %all-to-all-start.1 = ((bf16[2,64,6144]{2,1,0:T(8,128)(2,1)}), bf16[2,64,6144]{2,1,0:T(8,128)(2,1)S(1)}, u32[]{:S(2)}, u32[]{:S(2)}) async-start(bf16[2,64,6144]{2,1,0:T(8,128)(2,1)} %bitcast.21), calls=%async_computation.2 | async-start | bytes 3145728 | tf_op jit(solution)/shard_map/all_to_all | solution.py:83
  92.3 88.0 %reduce-scatter.5.cloned.1.call-start = ((), (), s32[]{:S(2)}) async-start(), calls=%async_computation.6 | async-start | bytes 3342336 | tf_op jit(solution)/shard_map/reduce_scatter | solution.py:87
  109.9 1.4 copy-start.2
  113.5 66.8 %copy-start.3 = (f32[64,768]{1,0:T(8,128)S(1)}, f32[64,768]{1,0:T(8,128)}, u32[]{:S(2)}) copy-start(f32[64,768]{1,0:T(8,128)} %param.10) | copy-start | bytes 589828
  113.5 66.8 %copy-start.4 = (f32[64,768]{1,0:T(8,128)S(1)}, f32[64,768]{1,0:T(8,128)}, u32[]{:S(2)}) copy-start(f32[64,768]{1,0:T(8,128)} %param.11) | copy-start | bytes 589828
  113.6 110.5 %all-gather.2.cloned.1.call-start = ((), (), s32[]{:S(2)}) async-start(), calls=%async_computation.7 | async-start | bytes 1671168 | tf_op jit(solution)/shard_map/all_gather | solution.py:98
Sparse Core Ops, SparseCore 0:
  39.6 10.5 reduce-scatter.2
  53.1 27.5 all-reduce.1
  113.7 66.5 reduce-scatter.4
  183.0 41.1 all-gather.1
where the time goes:
time: 234 us; the launch traced here: 233 us
  waiting for transfers between devices  164 us (70%)
  blocking collectives  22.4 us (10%)
  between operations  13.9 us (6%)
  matrix products  9.21 us (4%)
  starting transfers between devices  8.44 us (4%)
  other arithmetic  7.9 us (3%)
  local copies, waits for them, and re-layouts  6.92 us (3%)
    reduce_scatter x1, waiting for transfers between devices, shards(): shares = lax.psum_scatter(gradient, 'tgt', scatter_dimension=1, tiled=True)  66.7 us
    all_gather x1, waiting for transfers between devices, shards(): new_support = lax.all_gather(new_slab, 'tgt', axis=1, tiled=True)  42 us
    psum x1, waiting for transfers between devices, shards(): lax.psum(partial_pred.astype(jnp.bfloat16), 'sup').astype(jnp.float32)  27.9 us
    psum x1, blocking collectives, shards(): target_diag = lax.psum(row_squares(targets), 'sup') / pixels + bias_var  19 us
    all_to_all x1, waiting for transfers between devices, shards(): lax.all_to_all(slab_grad.astype(jnp.bfloat16), 'sup', split_axis=0, conca...  17.2 us
    reduce_scatter x1, waiting for transfers between devices, shards(): lax.psum_scatter(partial_cross.astype(jnp.bfloat16), 'sup', scatter_dimen...  10.6 us
  transfers between devices with their start and end apart: 6, of which 5 were waited for; matrix products, arithmetic and copies ran while one was open for 1% of the time, Pallas kernels for 0%

commit v1 on v0

--- a/solution.py
+++ b/solution.py
@@ -1,8 +1,11 @@
+import functools
 import math
 
 import jax
 import jax.numpy as jnp
 from jax import lax
+from jax.experimental import pallas as pl
+from jax.experimental.pallas import tpu as pltpu
 from jax.sharding import PartitionSpec as P
 
 DEPTH = 3
@@ -99,9 +102,459 @@
     return (new_support, new_first, new_second)
 
 
+MESH = pl.DeviceIdType.MESH
+f32 = jnp.float32
+bf16 = jnp.bfloat16
+
+
+@jax.custom_jvp
+def arcsine(x):
+    a = jnp.abs(x)
+    big = a > 0.5
+    z = jnp.where(big, 0.5 * (1.0 - a), a * a)
+    s = jnp.where(big, jnp.sqrt(z), a)
+    p = 4.2163199048e-2 * z + 2.4181311049e-2
+    p = p * z + 4.5470025998e-2
+    p = p * z + 7.4953002686e-2
+    p = p * z + 1.6666752422e-1
+    p = p * z * s + s
+    r = jnp.where(big, math.pi / 2.0 - 2.0 * p, p)
+    return jnp.where(x < 0.0, -r, r)
+
+
+@arcsine.defjvp
+def arcsine_jvp(primals, tangents):
+    (x,) = primals
+    (t,) = tangents
+    return arcsine(x), t * lax.rsqrt(1.0 - x * x)
+
+
+def tangent_tile(cross, target_diag, support_diag):
+    tangent = cross
+    current = cross
+    left = target_diag
+    right = support_diag
+    for _ in range(DEPTH):
+        product = (1.0 + 2.0 * left) * (1.0 + 2.0 * right)
+        slope = 4.0 / math.pi * lax.rsqrt(product - 4.0 * current * current)
+        current = 2.0 / math.pi * arcsine(2.0 * current * lax.rsqrt(product)) + bias_var
+        tangent = current + slope * tangent
+        left = 2.0 / math.pi * arcsine(2.0 * left / (1.0 + 2.0 * left)) + bias_var
+        right = 2.0 / math.pi * arcsine(2.0 * right / (1.0 + 2.0 * right)) + bias_var
+    return tangent
+
+
+def to_row(col, offset, lanes):
+    shape = (col.shape[0], lanes)
+    hit = lax.broadcasted_iota(jnp.int32, shape, 1) == lax.broadcasted_iota(jnp.int32, shape, 0) + offset
+    return jnp.sum(jnp.where(hit, col, 0.0), axis=0, keepdims=True)
+
+
+def to_col(row, count):
+    shape = (count, row.shape[1])
+    hit = lax.broadcasted_iota(jnp.int32, shape, 1) == lax.broadcasted_iota(jnp.int32, shape, 0)
+    return jnp.sum(jnp.where(hit, row, 0.0), axis=1, keepdims=True)
+
+
+SLAB, FWD, DIAG, CROSS, WEIGHTS, LOW, NORM = 0, 4, 8, 9, 10, 11, 12
+PAIR, HALF_Y, HALF_Z, LATE_Z, LATE_Y, LAST_X, LAST_Z, LAST_A = 13, 17, 19, 21, 22, 23, 24, 25
+GAT = 26
+MESSAGES = 45
+
+
+def step_kernel(
+    scale, pixels,
+    t_hbm, s_hbm, w_hbm, labels_ref, m1_ref, m2_ref,
+    out_hbm, n1_ref, n2_ref,
+    t_v, slab, sup_v, lw, tacc, dmsg_s, dmsg_r, cacc, cmsg_s, cmsg_r, low, nmsg_s, nmsg_r,
+    s1, keep, r1, s2y, s2z, r2y, r2z, s3, r3, own, s4, r4, ns,
+    send_sem, recv_sem, local_sem, out_sem,
+):
+    tgt = lax.axis_index("tgt")
+    x = lax.axis_index("sup")
+    core = lax.rem(tgt, 2)
+    yy = lax.rem(tgt // 2, 2)
+    z0 = lax.rem(tgt // 4, 2)
+    z1 = tgt // 8
+    sib_t = tgt + 1 - 2 * core
+    y_t = tgt + 2 - 4 * yy
+    z0_t = tgt + 4 - 8 * z0
+    z1_t = tgt + 8 - 16 * z1
+    SIB, YP, ZP, ZF, XP, AN = (sib_t, x), (y_t, x), (z0_t, x), (z1_t, x), (tgt, 1 - x), (z1_t, 1 - x)
+
+    images, width = n1_ref.shape
+    rows, half = t_v.shape
+    mine_rows = rows // 2
+    lanes = slab.shape[0]
+
+    def remote(src, dst, number, device):
+        return pltpu.make_async_remote_copy(
+            src_ref=src, dst_ref=dst, send_sem=send_sem.at[number], recv_sem=recv_sem.at[number],
+            device_id=device, device_id_type=MESH,
+        )
+
+    started = []
+
+    def send(src, dst, number, device):
+        copy = remote(src, dst, number, device)
+        copy.start()
+        started.append(copy)
+
+    def arrived(dst, number, device):
+        remote(dst, dst, number, device).wait_recv()
+
+    def aligned(value, by):
+        return pl.multiple_of(value, by)
+
+    my_row = aligned(x * images, images)
+    peer_row = aligned((1 - x) * images, images)
+
+    load_t = pltpu.make_async_copy(t_hbm, t_v, local_sem.at[0])
+    load_s = pltpu.make_async_copy(s_hbm, sup_v, local_sem.at[1])
+    load_o = pltpu.make_async_copy(
+        s_hbm.at[:, pl.ds(aligned(x * half, width), half)], slab.at[pl.ds(my_row, images), :], local_sem.at[2]
+    )
+    load_w = pltpu.make_async_copy(w_hbm, lw.at[pl.ds(my_row, images), :], local_sem.at[3])
+    load_t.start()
+    load_s.start()
+    load_o.start()
+    load_w.start()
+
+    barrier = pltpu.get_barrier_semaphore()
+    for device in (SIB, YP, ZP, ZF, XP, AN):
+        pl.semaphore_signal(barrier, inc=1, device_id=device, device_id_type=MESH)
+    pl.semaphore_wait(barrier, 6)
+
+    def piece(which, index):
+        return aligned((which * 4 + index) * width, width)
+
+    for p in range(4):
+        send(
+            s_hbm.at[:, pl.ds(aligned((1 - x) * half + (core * 4 + p) * width, width), width)],
+            slab.at[pl.ds(my_row, images), pl.ds(piece(core, p), width)],
+            SLAB + p, XP,
+        )
+
+    load_s.wait()
+
+    def support_squares(i, acc):
+        block = sup_v[:, pl.ds(aligned(i * width, width), width)].astype(f32)
+        block = block * block
+        for k in range(width // 128):
+            acc = acc + block[:, k * 128 : (k + 1) * 128]
+        return acc
+
+    sacc = lax.fori_loop(0, pixels // width, support_squares, jnp.zeros((images, 128), f32))
+    s_row = to_row(jnp.sum(sacc, axis=1, keepdims=True), x * images, lanes)
+    load_t.wait()
+    tacc[...] = jnp.zeros_like(tacc)
+
+    def target_squares(i, carry):
+        block = t_v[:, pl.ds(aligned(i * width, width), width)].astype(f32)
+        block = block * block
+        acc = tacc[...]
+        for k in range(width // 128):
+            acc = acc + block[:, k * 128 : (k + 1) * 128]
+        tacc[...] = acc
+        return carry
+
+    lax.fori_loop(0, half // width, target_squares, 0)
+    peer_first = aligned((1 - x) * mine_rows, mine_rows)
+    my_first = aligned(x * mine_rows, mine_rows)
+    peer_sq = jnp.sum(tacc[pl.ds(peer_first, mine_rows), :], axis=1, keepdims=True)
+    my_sq = jnp.sum(tacc[pl.ds(my_first, mine_rows), :], axis=1, keepdims=True)
+    dmsg_s[0:8, :] = jnp.broadcast_to(to_row(peer_sq, 0, lanes), (8, lanes))
+    dmsg_s[8:16, :] = jnp.broadcast_to(s_row, (8, lanes))
+    send(dmsg_s, dmsg_r, DIAG, XP)
+
+    load_o.wait()
+    cacc[...] = jnp.zeros_like(cacc)
+
+    def cross_piece(column):
+        cacc[...] += lax.dot_general(
+            t_v[:, pl.ds(column, width)], slab[:, pl.ds(column, width)], (((1,), (1,)), ((), ())),
+            preferred_element_type=f32,
+        )
+
+    for p in range(4):
+        here = slab.at[pl.ds(peer_row, images), pl.ds(piece(core, p), width)]
+        arrived(here, SLAB + p, XP)
+        send(here, here, FWD + p, SIB)
+        cross_piece(piece(core, p))
+        if p > 0:
+            arrived(slab.at[pl.ds(peer_row, images), pl.ds(piece(1 - core, p - 1), width)], FWD + p - 1, SIB)
+            cross_piece(piece(1 - core, p - 1))
+    arrived(slab.at[pl.ds(peer_row, images), pl.ds(piece(1 - core, 3), width)], FWD + 3, SIB)
+    cross_piece(piece(1 - core, 3))
+
+    cmsg_s[...] = cacc[pl.ds(peer_first, mine_rows), :].astype(bf16)
+    send(cmsg_s, cmsg_r, CROSS, XP)
+    send(w_hbm, lw.at[pl.ds(my_row, images), :], WEIGHTS, XP)
+
+    arrived(dmsg_r, DIAG, XP)
+    target_diag = (my_sq + to_col(dmsg_r[0:1, :], mine_rows)) / pixels + bias_var
+    support_diag = (s_row + dmsg_r[8:9, :]) / pixels + bias_var
+    arrived(cmsg_r, CROSS, XP)
+    cross = (cacc[pl.ds(my_first, mine_rows), :] + cmsg_r[...].astype(f32)) / pixels + bias_var
+
+    def kernel_of(cross_in, diag_in):
+        return tangent_tile(cross_in, target_diag, diag_in)
+
+    kernel, pullback = jax.vjp(kernel_of, cross, support_diag)
+    load_w.wait()
+    arrived(lw.at[pl.ds(peer_row, images), :], WEIGHTS, XP)
+    weights = lw[...]
+    predicted = jnp.dot(kernel.astype(bf16), weights, preferred_element_type=f32)
+    classes = lax.broadcasted_iota(jnp.int32, predicted.shape, 1)
+    onehot = (labels_ref[pl.ds(my_first, mine_rows), :] == classes).astype(f32)
+    residual = (predicted - onehot).astype(bf16)
+    kernel_grad = scale * lax.dot_general(
+        residual, weights, (((1,), (1,)), ((), ())), preferred_element_type=f32
+    )
+    cross_grad, norm_grad = pullback(kernel_grad)
+    mine_low = low.at[pl.ds(my_first, mine_rows), :]
+    mine_low[...] = cross_grad.astype(bf16)
+    nmsg_s[...] = jnp.broadcast_to(norm_grad, nmsg_s.shape)
+    send(mine_low, mine_low, LOW, XP)
+    send(nmsg_s, nmsg_r, NORM, XP)
+    arrived(low.at[pl.ds(peer_first, mine_rows), :], LOW, XP)
+    arrived(nmsg_r, NORM, XP)
+    norm_col = to_col(2.0 * (norm_grad + nmsg_r[0:1, :]), lanes)
+    grads = low[...]
+
+    order = ((1, 1), (0, 1), (1, 0), (0, 0))
+    chunk = 256 if width % 256 == 0 else 128
+
+    def slab_grad(index, other, store):
+        dz, dy = order[index]
+        number = (z0 + dz - 2 * dz * z0) * 4 + (yy + dy - 2 * dy * yy) * 2 + (1 - core if other else core)
+
+        def body(i, carry):
+            columns = pl.ds(aligned(number * width + i * chunk, chunk), chunk)
+            value = lax.dot_general(
+                grads, t_v[:, columns], (((0,), (0,)), ((), ())), preferred_element_type=f32
+            )
+            value = value + norm_col * slab[:, columns].astype(f32)
+            store(pl.ds(aligned(i * chunk, chunk), chunk), value)
+            return carry
+
+        lax.fori_loop(0, width // chunk, body, 0)
+
+    for k in range(4):
+        def store_sent(columns, value, k=k):
+            s1[k, :, columns] = value.astype(bf16)
+
+        slab_grad(k, True, store_sent)
+        send(s1.at[k], r1.at[k], PAIR + k, SIB)
+    for k in range(4):
+        def store_kept(columns, value, k=k):
+            keep[k, :, columns] = value
+
+        slab_grad(k, False, store_kept)
+
+    first = slice(0, images)
+    second = slice(images, 2 * images)
+
+    def pair_sum(k, part):
+        return keep[k, part, :] + r1[k, part, :].astype(f32)
+
+    arrived(r1.at[0], PAIR, SIB)
+    s2y[0] = pair_sum(0, first).astype(bf16)
+    send(s2y.at[0], r2y.at[0], HALF_Y, YP)
+    s2z[0] = pair_sum(0, second).astype(bf16)
+    send(s2z.at[0], r2z.at[0], HALF_Z, ZP)
+    arrived(r1.at[1], PAIR + 1, SIB)
+    s2y[1] = pair_sum(1, first).astype(bf16)
+    send(s2y.at[1], r2y.at[1], HALF_Y + 1, YP)
+    arrived(r1.at[2], PAIR + 2, SIB)
+    s2z[1] = pair_sum(2, second).astype(bf16)
+    send(s2z.at[1], r2z.at[1], HALF_Z + 1, ZP)
+
+    arrived(r2y.at[0], HALF_Y, YP)
+    s3[0] = (pair_sum(2, first) + r2y[0].astype(f32)).astype(bf16)
+    send(s3.at[0], r3.at[0], LATE_Z, ZP)
+    arrived(r2z.at[0], HALF_Z, ZP)
+    s3[1] = (pair_sum(1, second) + r2z[0].astype(f32)).astype(bf16)
+    send(s3.at[1], r3.at[1], LATE_Y, YP)
+    arrived(r1.at[3], PAIR + 3, SIB)
+    arrived(r2y.at[1], HALF_Y + 1, YP)
+    own[0] = pair_sum(3, first) + r2y[1].astype(f32)
+    arrived(r2z.at[1], HALF_Z + 1, ZP)
+    own[1] = pair_sum(3, second) + r2z[1].astype(f32)
+    arrived(r3.at[0], LATE_Z, ZP)
+    own[0] = own[0] + r3[0].astype(f32)
+    s4[0] = own[0].astype(bf16)
+    arrived(r3.at[1], LATE_Y, YP)
+    own[1] = own[1] + r3[1].astype(f32)
+    s4[1] = own[1].astype(bf16)
+
+    home = z1 == x
+    last_x = remote(s4.at[1 - x], r4.at[0], LAST_X, XP)
+    last_z = remote(s4.at[x], r4.at[1], LAST_Z, ZF)
+    last_a = remote(s4.at[1 - x], r4.at[1], LAST_A, AN)
+
+    @pl.when(home)
+    def _():
+        last_x.start()
+        last_z.wait_recv()
+        keep[0, first, :] = own[x] + r4[1].astype(f32)
+        last_x.wait_send()
+
+    @pl.when(jnp.logical_not(home))
+    def _():
+        last_a.start()
+        last_z.start()
+        last_x.wait_recv()
+        last_a.wait_recv()
+        keep[0, first, :] = r4[0].astype(f32) + r4[1].astype(f32)
+        last_a.wait_send()
+        last_z.wait_send()
+
+    def block(ref, index, part=slice(None)):
+        return ref.at[part, pl.ds(aligned(index * width, width), width)]
+
+    gradient = keep[0, first, :] / pixels
+    new_first = first_decay * m1_ref[...] + (1.0 - first_decay) * gradient
+    new_second = second_decay * m2_ref[...] + (1.0 - second_decay) * gradient * gradient
+    update = learning_rate * (new_first / first_fix) / (jnp.sqrt(new_second / second_fix) + adam_eps)
+    mine = pl.ds(aligned(tgt * width, width), width)
+    ns[:, mine] = (sup_v[:, mine].astype(f32) - update).astype(bf16)
+    n1_ref[...] = new_first
+    n2_ref[...] = new_second
+
+    low_half, high_half = slice(0, images // 2), slice(images // 2, images)
+    z1y_t = y_t + z1_t - tgt
+    z1z0_t = z0_t + z1_t - tgt
+    d_t = y_t + z0_t - tgt
+    z1d_t = d_t + z1_t - tgt
+    swap = sib_t - tgt
+
+    def pass_on(index, number, device, part=slice(None)):
+        send(block(ns, index, part), block(ns, index, part), number, device)
+
+    def came(index, number, device, part=slice(None)):
+        arrived(block(ns, index, part), number, device)
+
+    pass_on(tgt, GAT, ZF)
+    pass_on(tgt, GAT + 1, YP)
+    pass_on(tgt, GAT + 2, ZP)
+    pass_on(tgt, GAT + 3, SIB)
+    came(z1_t, GAT, ZF)
+    pass_on(z1_t, GAT + 4, YP)
+    pass_on(z1_t, GAT + 5, ZP)
+    pass_on(z1_t, GAT + 6, SIB)
+    came(y_t, GAT + 1, YP)
+    pass_on(y_t, GAT + 7, ZP, high_half)
+    pass_on(y_t, GAT + 8, SIB)
+    came(z0_t, GAT + 2, ZP)
+    pass_on(z0_t, GAT + 9, YP, low_half)
+    pass_on(z0_t, GAT + 10, SIB)
+    came(z1y_t, GAT + 4, YP)
+    pass_on(z1y_t, GAT + 11, ZP, high_half)
+    pass_on(z1y_t, GAT + 12, SIB)
+    came(z1z0_t, GAT + 5, ZP)
+    pass_on(z1z0_t, GAT + 13, YP, low_half)
+    pass_on(z1z0_t, GAT + 14, SIB)
+    came(d_t, GAT + 7, ZP, high_half)
+    pass_on(d_t, GAT + 15, SIB, high_half)
+    came(d_t, GAT + 9, YP, low_half)
+    pass_on(d_t, GAT + 16, SIB, low_half)
+    came(z1d_t, GAT + 11, ZP, high_half)
+    pass_on(z1d_t, GAT + 17, SIB, high_half)
+    came(z1d_t, GAT + 13, YP, low_half)
+    pass_on(z1d_t, GAT + 18, SIB, low_half)
+
+    came(tgt + swap, GAT + 3, SIB)
+    came(z1_t + swap, GAT + 6, SIB)
+    came(y_t + swap, GAT + 8, SIB)
+    came(z0_t + swap, GAT + 10, SIB)
+    came(z1y_t + swap, GAT + 12, SIB)
+    came(z1z0_t + swap, GAT + 14, SIB)
+    came(d_t + swap, GAT + 15, SIB, high_half)
+    came(d_t + swap, GAT + 16, SIB, low_half)
+    came(z1d_t + swap, GAT + 17, SIB, high_half)
+    came(z1d_t + swap, GAT + 18, SIB, low_half)
+    store = pltpu.make_async_copy(ns, out_hbm, out_sem)
+    store.start()
+    for copy in started:
+        copy.wait_send()
+    store.wait()
+
+
+def fused(targets, support, label_weights, labels, first_moment, second_moment):
+    rows, half = targets.shape
+    images, pixels = support.shape
+    width = first_moment.shape[1]
+    classes = label_weights.shape[1]
+    target_count = rows * lax.axis_size("tgt")
+    support_count = images * lax.axis_size("sup")
+    scale = 4.0 * pixels * math.sqrt(classes * support_count / target_count)
+    everyone, part = 2 * images, rows // 2
+    hbm = pl.BlockSpec(memory_space=pl.ANY)
+    vmem = pl.BlockSpec(memory_space=pltpu.VMEM)
+    return pl.pallas_call(
+        functools.partial(step_kernel, scale, pixels),
+        out_shape=(
+            jax.ShapeDtypeStruct(support.shape, bf16),
+            jax.ShapeDtypeStruct(first_moment.shape, f32),
+            jax.ShapeDtypeStruct(first_moment.shape, f32),
+        ),
+        in_specs=[hbm, hbm, hbm, vmem, vmem, vmem],
+        out_specs=(hbm, vmem, vmem),
+        scratch_shapes=[
+            pltpu.VMEM((rows, half), bf16),
+            pltpu.VMEM((everyone, half), bf16),
+            pltpu.VMEM((images, pixels), bf16),
+            pltpu.VMEM((everyone, classes), bf16),
+            pltpu.VMEM((rows, 128), f32),
+            pltpu.VMEM((16, everyone), f32),
+            pltpu.VMEM((16, everyone), f32),
+            pltpu.VMEM((rows, everyone), f32),
+            pltpu.VMEM((part, everyone), bf16),
+            pltpu.VMEM((part, everyone), bf16),
+            pltpu.VMEM((rows, everyone), bf16),
+            pltpu.VMEM((8, everyone), f32),
+            pltpu.VMEM((8, everyone), f32),
+            pltpu.VMEM((4, everyone, width), bf16),
+            pltpu.VMEM((4, everyone, width), f32),
+            pltpu.VMEM((4, everyone, width), bf16),
+            pltpu.VMEM((2, images, width), bf16),
+            pltpu.VMEM((2, images, width), bf16),
+            pltpu.VMEM((2, images, width), bf16),
+            pltpu.VMEM((2, images, width), bf16),
+            pltpu.VMEM((2, images, width), bf16),
+            pltpu.VMEM((2, images, width), bf16),
+            pltpu.VMEM((2, images, width), f32),
+            pltpu.VMEM((2, images, width), bf16),
+            pltpu.VMEM((2, images, width), bf16),
+            pltpu.VMEM((images, pixels), bf16),
+            pltpu.SemaphoreType.DMA((MESSAGES,)),
+            pltpu.SemaphoreType.DMA((MESSAGES,)),
+            pltpu.SemaphoreType.DMA((4,)),
+            pltpu.SemaphoreType.DMA,
+        ],
+        compiler_params=pltpu.CompilerParams(
+            collective_id=0, has_side_effects=True, vmem_limit_bytes=48 * 1024 * 1024
+        ),
+    )(targets, support, label_weights, labels[:, None], first_moment, second_moment)
+
+
+def pick(mesh):
+    groups, shares = mesh.shape["sup"], mesh.shape["tgt"]
+
+    def run(targets, support, label_weights, labels, first_moment, second_moment):
+        width = first_moment.shape[1]
+        fits = groups == 2 and shares == 16 and width % 128 == 0
+        fits = fits and targets.shape[0] % 32 == 0 and groups * support.shape[0] == 128
+        body = fused if fits else shards
+        return body(targets, support, label_weights, labels, first_moment, second_moment)
+
+    return run
+
+
 def solution(mesh):
     return jax.shard_map(
-        shards,
+        pick(mesh),
         mesh=mesh,
         in_specs=(
             P("tgt", "sup"),

time: 234 us -> 69.8 us (0.30)
  waiting for transfers between devices: 164 us -> 0 us
  Pallas kernels: 0 us -> 61.4 us
  blocking collectives: 22.4 us -> 0 us
  between operations: 13.9 us -> 0.66 us
  matrix products: 9.21 us -> 0 us
  starting transfers between devices: 8.44 us -> 0 us
  other arithmetic: 7.9 us -> 0 us
    reduce_scatter x2 -> x0, waiting for transfers between devices: 77.3 us -> none  [the longest x1 66.7 us: shards(): shares = lax.psum_scatter(gradient, 'tgt', scatter_dimension=1, tiled=True)]
    pallas_call x0 -> x1, Pallas kernels: none -> 61.4 us  [fused(): pl.pallas_call(functools.partial(step_kernel, scale, pixels), out_shape=(...]
    all_gather x1 -> x0, waiting for transfers between devices: 42 us -> none  [shards(): new_support = lax.all_gather(new_slab, 'tgt', axis=1, tiled=True)]
    psum x1 -> x0, waiting for transfers between devices: 27.9 us -> none  [shards(): lax.psum(partial_pred.astype(jnp.bfloat16), 'sup').astype(jnp.float32)]
    psum x1 -> x0, blocking collectives: 19 us -> none  [shards(): target_diag = lax.psum(row_squares(targets), 'sup') / pixels + bias_var]
    all_to_all x2 -> x0, waiting for transfers between devices: 17.2 us -> none  [the longest x1 17.2 us: shards(): lax.all_to_all(slab_grad.astype(jnp.bfloat16), 'sup', split_axis=0, conca...]
    dot_general x4 -> x0, matrix products: 9.21 us -> none  [the longest x1 3.13 us: shards(): lax.dot_general(targets, slabs, (((1,), (1,)), ((), ())), preferred_eleme...]
    all_to_all x2 -> x0, starting transfers between devices: 8.28 us -> none  [the longest x1 4.6 us: shards(): lax.all_to_all(support, 'sup', split_axis=1, concat_axis=0, tiled=True)]
  transfers between devices with their start and end apart: 6 -> 0, of which waited for: 5 -> 0; matrix products, arithmetic and copies ran while one was open for 1% -> 0% of each run, Pallas kernels for 0% -> 0%
where the time goes in v1:
time: 69.8 us; the launch traced here: 69.5 us
  Pallas kernels  61.4 us (88%)
  local copies, waits for them, and re-layouts  7.46 us (11%)
    pallas_call x1, Pallas kernels, fused(): pl.pallas_call(functools.partial(step_kernel, scale, pixels), out_shape=(...  61.4 us
    unnamed x11, local copies, waits for them, and re-layouts  6.66 us

profile of v1, /device:TPU:1, one launch (start us, length us, event | category | flops | bytes accessed | tf_op | source)
XLA Modules:
  0.0 69.5 jit_solution(13923014154931159337)
XLA Ops:
  0.6 0.8 %copy.9.labels_ref = s32[224,1]{1,0:T(8,128)S(1)} copy(s32[224,1]{0,1:T(1,128)} %bitcast.1) | data formatting | bytes 1792 | tf_op jit(solution)/shard_map/broadcast_in_dim | solution.py:539
  1.4 0.0 copy-start
  1.4 1.4 %copy-done = bf16[64,12288]{1,0:T(8,128)(2,1)S(1)} copy-done((bf16[64,12288]{1,0:T(8,128)(2,1)S(1)}, bf16[64,12288]{1,0:T(8,128)(2,1)}, u32[]{:S(2)}) %copy-start) | copy-done | bytes 1572888
  2.8 0.0 copy-start.1
  2.9 0.9 %copy-done.1 = f32[64,768]{1,0:T(8,128)S(1)} copy-done((f32[64,768]{1,0:T(8,128)S(1)}, f32[64,768]{1,0:T(8,128)}, u32[]{:S(2)}) %copy-start.1) | copy-done | bytes 196632
  3.8 0.0 copy-start.2
  3.8 0.9 %copy-done.2 = f32[64,768]{1,0:T(8,128)S(1)} copy-done((f32[64,768]{1,0:T(8,128)S(1)}, f32[64,768]{1,0:T(8,128)}, u32[]{:S(2)}) %copy-start.2) | copy-done | bytes 196632
  4.7 0.0 copy-start.3
  4.7 0.9 %copy-done.3 = bf16[64,1000]{1,0:T(8,128)(2,1)S(1)} copy-done((bf16[64,1000]{1,0:T(8,128)(2,1)S(1)}, bf16[64,1000]{1,0:T(8,128)(2,1)}, u32[]{:S(2)}) %copy-start.3) | copy-done | bytes 128024
  5.6 61.4 %shard_map.85 = (bf16[64,12288]{1,0:T(8,128)(2,1)S(1)}, f32[64,768]{1,0:T(8,128)S(1)}, f32[64,768]{1,0:T(8,128)S(1)}) custom-call(bf16[224,6144]{1,0:T(8,128)(2,1)} %t_hbm.1, bf16[64,12288]{1,0:T(8,128)(2,1)S(1)} %copy-done, bf16[64,1000]{1,0:T(8,128)(2,1)S(1)} %copy-done.3, s32[224,1]{1,0:T(8,128)S(1)} %copy.9.labels_ref, f32[64,768]{1,0:T(8,128)S(1)} %copy-done.1, ...), custom_call_target="tpu_custom_call" | custom-call | tf_op jit(solution)/shard_map/pallas_call | solution.py:495
  67.0 1.1 %copy.13 = bf16[64,12288]{1,0:T(8,128)(2,1)} copy(bf16[64,12288]{1,0:T(8,128)(2,1)S(1)} %get-tuple-element.6) | data formatting | bytes 3145728
  68.2 0.7 copy.14
  68.9 0.7 copy.15
Async XLA Ops:
  1.4 1.4 %copy-start = (bf16[64,12288]{1,0:T(8,128)(2,1)S(1)}, bf16[64,12288]{1,0:T(8,128)(2,1)}, u32[]{:S(2)}) copy-start(bf16[64,12288]{1,0:T(8,128)(2,1)} %s_hbm.1) | copy-start | bytes 4718596
  2.8 0.9 %copy-start.1 = (f32[64,768]{1,0:T(8,128)S(1)}, f32[64,768]{1,0:T(8,128)}, u32[]{:S(2)}) copy-start(f32[64,768]{1,0:T(8,128)} %m1_ref.1) | copy-start | bytes 589828
  3.8 0.9 %copy-start.2 = (f32[64,768]{1,0:T(8,128)S(1)}, f32[64,768]{1,0:T(8,128)}, u32[]{:S(2)}) copy-start(f32[64,768]{1,0:T(8,128)} %m2_ref.1) | copy-start | bytes 589828
  4.7 0.9 %copy-start.3 = (bf16[64,1000]{1,0:T(8,128)(2,1)S(1)}, bf16[64,1000]{1,0:T(8,128)(2,1)}, u32[]{:S(2)}) copy-start(bf16[64,1000]{1,0:T(8,128)(2,1)} %w_hbm.1) | copy-start | bytes 384004

commit v2 on v1

--- a/solution.py
+++ b/solution.py
@@ -150,24 +150,24 @@
     return jnp.sum(jnp.where(hit, col, 0.0), axis=0, keepdims=True)
 
 
-def to_col(row, count):
+def to_col(row, count, offset=0):
     shape = (count, row.shape[1])
-    hit = lax.broadcasted_iota(jnp.int32, shape, 1) == lax.broadcasted_iota(jnp.int32, shape, 0)
+    hit = lax.broadcasted_iota(jnp.int32, shape, 1) == lax.broadcasted_iota(jnp.int32, shape, 0) + offset
     return jnp.sum(jnp.where(hit, row, 0.0), axis=1, keepdims=True)
 
 
 SLAB, FWD, DIAG, CROSS, WEIGHTS, LOW, NORM = 0, 4, 8, 9, 10, 11, 12
 PAIR, HALF_Y, HALF_Z, LATE_Z, LATE_Y, LAST_X, LAST_Z, LAST_A = 13, 17, 19, 21, 22, 23, 24, 25
 GAT = 26
-MESSAGES = 45
+MESSAGES = 51
 
 
 def step_kernel(
     scale, pixels,
-    t_hbm, s_hbm, w_hbm, labels_ref, m1_ref, m2_ref,
+    t_hbm, s_hbm, w_hbm, labels_hbm, m1_hbm, m2_hbm,
     out_hbm, n1_ref, n2_ref,
     t_v, slab, sup_v, lw, tacc, dmsg_s, dmsg_r, cacc, cmsg_s, cmsg_r, low, nmsg_s, nmsg_r,
-    s1, keep, r1, s2y, s2z, r2y, r2z, s3, r3, own, s4, r4, ns,
+    s1, keep, r1, s2y, s2z, r2y, r2z, s3, r3, own, s4, r4, ns, labels_ref, m1_ref, m2_ref,
     send_sem, recv_sem, local_sem, out_sem,
 ):
     tgt = lax.axis_index("tgt")
@@ -219,6 +219,12 @@
     load_s.start()
     load_o.start()
     load_w.start()
+    load_l = pltpu.make_async_copy(labels_hbm, labels_ref, local_sem.at[4])
+    load_1 = pltpu.make_async_copy(m1_hbm, m1_ref, local_sem.at[5])
+    load_2 = pltpu.make_async_copy(m2_hbm, m2_ref, local_sem.at[6])
+    load_l.start()
+    load_1.start()
+    load_2.start()
 
     barrier = pltpu.get_barrier_semaphore()
     for device in (SIB, YP, ZP, ZF, XP, AN):
@@ -228,12 +234,16 @@
     def piece(which, index):
         return aligned((which * 4 + index) * width, width)
 
-    for p in range(4):
+    seat = 2 * yy + z0
+    turn = (seat, 3 - seat, seat + 2 - 4 * yy, seat + 1 - 2 * z0)
+    source = (XP, XP, YP, ZP)
+    for p in range(2):
         send(
-            s_hbm.at[:, pl.ds(aligned((1 - x) * half + (core * 4 + p) * width, width), width)],
-            slab.at[pl.ds(my_row, images), pl.ds(piece(core, p), width)],
+            s_hbm.at[:, pl.ds(aligned((1 - x) * half + (core * 4 + turn[p]) * width, width), width)],
+            slab.at[pl.ds(my_row, images), pl.ds(aligned((core * 4 + turn[p]) * width, width), width)],
             SLAB + p, XP,
         )
+    send(w_hbm, lw.at[pl.ds(my_row, images), :], WEIGHTS, XP)
 
     load_s.wait()
 
@@ -263,6 +273,8 @@
     my_first = aligned(x * mine_rows, mine_rows)
     peer_sq = jnp.sum(tacc[pl.ds(peer_first, mine_rows), :], axis=1, keepdims=True)
     my_sq = jnp.sum(tacc[pl.ds(my_first, mine_rows), :], axis=1, keepdims=True)
+    load_l.wait()
+    label_col = to_col(labels_ref[...].astype(f32), mine_rows, x * mine_rows)
     dmsg_s[0:8, :] = jnp.broadcast_to(to_row(peer_sq, 0, lanes), (8, lanes))
     dmsg_s[8:16, :] = jnp.broadcast_to(s_row, (8, lanes))
     send(dmsg_s, dmsg_r, DIAG, XP)
@@ -277,19 +289,23 @@
         )
 
     for p in range(4):
-        here = slab.at[pl.ds(peer_row, images), pl.ds(piece(core, p), width)]
-        arrived(here, SLAB + p, XP)
+        here = slab.at[pl.ds(peer_row, images), pl.ds(piece(core, turn[p]), width)]
+        arrived(here, SLAB + p, source[p])
+        if p == 0:
+            send(here, here, SLAB + 2, YP)
+            send(here, here, SLAB + 3, ZP)
         send(here, here, FWD + p, SIB)
-        cross_piece(piece(core, p))
+        cross_piece(piece(core, turn[p]))
         if p > 0:
-            arrived(slab.at[pl.ds(peer_row, images), pl.ds(piece(1 - core, p - 1), width)], FWD + p - 1, SIB)
-            cross_piece(piece(1 - core, p - 1))
-    arrived(slab.at[pl.ds(peer_row, images), pl.ds(piece(1 - core, 3), width)], FWD + 3, SIB)
-    cross_piece(piece(1 - core, 3))
+            there = piece(1 - core, turn[p - 1])
+            arrived(slab.at[pl.ds(peer_row, images), pl.ds(there, width)], FWD + p - 1, SIB)
+            cross_piece(there)
+    there = piece(1 - core, turn[3])
+    arrived(slab.at[pl.ds(peer_row, images), pl.ds(there, width)], FWD + 3, SIB)
+    cross_piece(there)
 
     cmsg_s[...] = cacc[pl.ds(peer_first, mine_rows), :].astype(bf16)
     send(cmsg_s, cmsg_r, CROSS, XP)
-    send(w_hbm, lw.at[pl.ds(my_row, images), :], WEIGHTS, XP)
 
     arrived(dmsg_r, DIAG, XP)
     target_diag = (my_sq + to_col(dmsg_r[0:1, :], mine_rows)) / pixels + bias_var
@@ -306,7 +322,7 @@
     weights = lw[...]
     predicted = jnp.dot(kernel.astype(bf16), weights, preferred_element_type=f32)
     classes = lax.broadcasted_iota(jnp.int32, predicted.shape, 1)
-    onehot = (labels_ref[pl.ds(my_first, mine_rows), :] == classes).astype(f32)
+    onehot = (label_col == classes.astype(f32)).astype(f32)
     residual = (predicted - onehot).astype(bf16)
     kernel_grad = scale * lax.dot_general(
         residual, weights, (((1,), (1,)), ((), ())), preferred_element_type=f32
@@ -340,35 +356,44 @@
 
         lax.fori_loop(0, width // chunk, body, 0)
 
-    for k in range(4):
-        def store_sent(columns, value, k=k):
-            s1[k, :, columns] = value.astype(bf16)
-
-        slab_grad(k, True, store_sent)
-        send(s1.at[k], r1.at[k], PAIR + k, SIB)
-    for k in range(4):
-        def store_kept(columns, value, k=k):
-            keep[k, :, columns] = value
-
-        slab_grad(k, False, store_kept)
-
     first = slice(0, images)
     second = slice(images, 2 * images)
 
     def pair_sum(k, part):
         return keep[k, part, :] + r1[k, part, :].astype(f32)
 
+    def give(k):
+        def store(columns, value):
+            s1[k, :, columns] = value.astype(bf16)
+
+        slab_grad(k, True, store)
+        send(s1.at[k], r1.at[k], PAIR + k, SIB)
+
+    def hold(k):
+        def store(columns, value):
+            keep[k, :, columns] = value
+
+        slab_grad(k, False, store)
+
+    give(0)
+    give(1)
+    hold(0)
     arrived(r1.at[0], PAIR, SIB)
     s2y[0] = pair_sum(0, first).astype(bf16)
     send(s2y.at[0], r2y.at[0], HALF_Y, YP)
     s2z[0] = pair_sum(0, second).astype(bf16)
     send(s2z.at[0], r2z.at[0], HALF_Z, ZP)
+    give(2)
+    hold(1)
     arrived(r1.at[1], PAIR + 1, SIB)
     s2y[1] = pair_sum(1, first).astype(bf16)
     send(s2y.at[1], r2y.at[1], HALF_Y + 1, YP)
+    hold(2)
     arrived(r1.at[2], PAIR + 2, SIB)
     s2z[1] = pair_sum(2, second).astype(bf16)
     send(s2z.at[1], r2z.at[1], HALF_Z + 1, ZP)
+    give(3)
+    hold(3)
 
     arrived(r2y.at[0], HALF_Y, YP)
     s3[0] = (pair_sum(2, first) + r2y[0].astype(f32)).astype(bf16)
@@ -413,6 +438,8 @@
     def block(ref, index, part=slice(None)):
         return ref.at[part, pl.ds(aligned(index * width, width), width)]
 
+    load_1.wait()
+    load_2.wait()
     gradient = keep[0, first, :] / pixels
     new_first = first_decay * m1_ref[...] + (1.0 - first_decay) * gradient
     new_second = second_decay * m2_ref[...] + (1.0 - second_decay) * gradient * gradient
@@ -435,45 +462,52 @@
     def came(index, number, device, part=slice(None)):
         arrived(block(ns, index, part), number, device)
 
-    pass_on(tgt, GAT, ZF)
-    pass_on(tgt, GAT + 1, YP)
-    pass_on(tgt, GAT + 2, ZP)
-    pass_on(tgt, GAT + 3, SIB)
-    came(z1_t, GAT, ZF)
-    pass_on(z1_t, GAT + 4, YP)
-    pass_on(z1_t, GAT + 5, ZP)
-    pass_on(z1_t, GAT + 6, SIB)
-    came(y_t, GAT + 1, YP)
-    pass_on(y_t, GAT + 7, ZP, high_half)
-    pass_on(y_t, GAT + 8, SIB)
-    came(z0_t, GAT + 2, ZP)
-    pass_on(z0_t, GAT + 9, YP, low_half)
-    pass_on(z0_t, GAT + 10, SIB)
-    came(z1y_t, GAT + 4, YP)
-    pass_on(z1y_t, GAT + 11, ZP, high_half)
-    pass_on(z1y_t, GAT + 12, SIB)
-    came(z1z0_t, GAT + 5, ZP)
-    pass_on(z1z0_t, GAT + 13, YP, low_half)
-    pass_on(z1z0_t, GAT + 14, SIB)
-    came(d_t, GAT + 7, ZP, high_half)
+    halves = (low_half, high_half)
+    pass_on(tgt, GAT, ZF, low_half)
+    pass_on(tgt, GAT + 1, ZF, high_half)
+    pass_on(tgt, GAT + 2, YP)
+    pass_on(tgt, GAT + 3, ZP)
+    pass_on(tgt, GAT + 4, SIB)
+    came(y_t, GAT + 2, YP)
+    pass_on(y_t, GAT + 5, ZP, high_half)
+    pass_on(y_t, GAT + 6, SIB)
+    came(z0_t, GAT + 3, ZP)
+    pass_on(z0_t, GAT + 7, YP, low_half)
+    pass_on(z0_t, GAT + 8, SIB)
+    for h in (0, 1):
+        came(z1_t, GAT + h, ZF, halves[h])
+        pass_on(z1_t, GAT + 9 + h, YP, halves[h])
+        pass_on(z1_t, GAT + 11 + h, ZP, halves[h])
+        pass_on(z1_t, GAT + 13 + h, SIB, halves[h])
+    came(d_t, GAT + 5, ZP, high_half)
     pass_on(d_t, GAT + 15, SIB, high_half)
-    came(d_t, GAT + 9, YP, low_half)
+    came(d_t, GAT + 7, YP, low_half)
     pass_on(d_t, GAT + 16, SIB, low_half)
-    came(z1d_t, GAT + 11, ZP, high_half)
-    pass_on(z1d_t, GAT + 17, SIB, high_half)
-    came(z1d_t, GAT + 13, YP, low_half)
-    pass_on(z1d_t, GAT + 18, SIB, low_half)
-
-    came(tgt + swap, GAT + 3, SIB)
-    came(z1_t + swap, GAT + 6, SIB)
-    came(y_t + swap, GAT + 8, SIB)
-    came(z0_t + swap, GAT + 10, SIB)
-    came(z1y_t + swap, GAT + 12, SIB)
-    came(z1z0_t + swap, GAT + 14, SIB)
+    for h in (0, 1):
+        came(z1z0_t, GAT + 11 + h, ZP, halves[h])
+        if h == 0:
+            pass_on(z1z0_t, GAT + 17, YP, low_half)
+        pass_on(z1z0_t, GAT + 18 + h, SIB, halves[h])
+        came(z1y_t, GAT + 9 + h, YP, halves[h])
+        if h == 1:
+            pass_on(z1y_t, GAT + 20, ZP, high_half)
+        pass_on(z1y_t, GAT + 21 + h, SIB, halves[h])
+    came(z1d_t, GAT + 17, YP, low_half)
+    pass_on(z1d_t, GAT + 23, SIB, low_half)
+    came(z1d_t, GAT + 20, ZP, high_half)
+    pass_on(z1d_t, GAT + 24, SIB, high_half)
+
+    came(tgt + swap, GAT + 4, SIB)
+    came(y_t + swap, GAT + 6, SIB)
+    came(z0_t + swap, GAT + 8, SIB)
     came(d_t + swap, GAT + 15, SIB, high_half)
     came(d_t + swap, GAT + 16, SIB, low_half)
-    came(z1d_t + swap, GAT + 17, SIB, high_half)
-    came(z1d_t + swap, GAT + 18, SIB, low_half)
+    for h in (0, 1):
+        came(z1_t + swap, GAT + 13 + h, SIB, halves[h])
+        came(z1z0_t + swap, GAT + 18 + h, SIB, halves[h])
+        came(z1y_t + swap, GAT + 21 + h, SIB, halves[h])
+    came(z1d_t + swap, GAT + 23, SIB, low_half)
+    came(z1d_t + swap, GAT + 24, SIB, high_half)
     store = pltpu.make_async_copy(ns, out_hbm, out_sem)
     store.start()
     for copy in started:
@@ -490,7 +524,7 @@
     support_count = images * lax.axis_size("sup")
     scale = 4.0 * pixels * math.sqrt(classes * support_count / target_count)
     everyone, part = 2 * images, rows // 2
-    hbm = pl.BlockSpec(memory_space=pl.ANY)
+    hbm = pl.BlockSpec(memory_space=pltpu.HBM)
     vmem = pl.BlockSpec(memory_space=pltpu.VMEM)
     return pl.pallas_call(
         functools.partial(step_kernel, scale, pixels),
@@ -499,8 +533,8 @@
             jax.ShapeDtypeStruct(first_moment.shape, f32),
             jax.ShapeDtypeStruct(first_moment.shape, f32),
         ),
-        in_specs=[hbm, hbm, hbm, vmem, vmem, vmem],
-        out_specs=(hbm, vmem, vmem),
+        in_specs=[hbm] * 6,
+        out_specs=(pl.BlockSpec(memory_space=pl.ANY), vmem, vmem),
         scratch_shapes=[
             pltpu.VMEM((rows, half), bf16),
             pltpu.VMEM((everyone, half), bf16),
@@ -528,15 +562,18 @@
             pltpu.VMEM((2, images, width), bf16),
             pltpu.VMEM((2, images, width), bf16),
             pltpu.VMEM((images, pixels), bf16),
+            pltpu.VMEM((1, rows), jnp.int32),
+            pltpu.VMEM((images, width), f32),
+            pltpu.VMEM((images, width), f32),
             pltpu.SemaphoreType.DMA((MESSAGES,)),
             pltpu.SemaphoreType.DMA((MESSAGES,)),
-            pltpu.SemaphoreType.DMA((4,)),
+            pltpu.SemaphoreType.DMA((7,)),
             pltpu.SemaphoreType.DMA,
         ],
         compiler_params=pltpu.CompilerParams(
-            collective_id=0, has_side_effects=True, vmem_limit_bytes=48 * 1024 * 1024
+            collective_id=0, has_side_effects=True, vmem_limit_bytes=60000000
         ),
-    )(targets, support, label_weights, labels[:, None], first_moment, second_moment)
+    )(targets, support, label_weights, labels[None, :], first_moment, second_moment)
 
 
 def pick(mesh):

time: 69.8 us -> 65.4 us (0.937)
  local copies, waits for them, and re-layouts: 7.46 us -> 4.06 us
  Pallas kernels: 61.4 us -> 60.5 us
    unnamed x11 -> x7, local copies, waits for them, and re-layouts: 6.66 us -> 4.06 us
    pallas_call x1, Pallas kernels: 61.4 us -> 60.5 us  [fused(): pl.pallas_call(functools.partial(step_kernel, scale, pixels), out_shape=(...]
    broadcast_in_dim x1 -> x0, local copies, waits for them, and re-layouts: 0.8 us -> none  [fused(): labels[:, None]]
where the time goes in v2:
time: 65.4 us; the launch traced here: 65.2 us
  Pallas kernels  60.5 us (93%)
  local copies, waits for them, and re-layouts  4.06 us (6%)
  between operations  0.66 us (1%)
    pallas_call x1, Pallas kernels, fused(): pl.pallas_call(functools.partial(step_kernel, scale, pixels), out_shape=(...  60.5 us
    unnamed x7, local copies, waits for them, and re-layouts  4.06 us

profile of v2, /device:TPU:1, one launch (start us, length us, event | category | flops | bytes accessed | tf_op | source)
XLA Modules:
  0.0 65.2 jit_solution(15900840486907466863)
XLA Ops:
  0.6 60.5 %shard_map.85 = (bf16[64,12288]{1,0:T(8,128)(2,1)}, f32[64,768]{1,0:T(8,128)}, f32[64,768]{1,0:T(8,128)}) custom-call(bf16[224,6144]{1,0:T(8,128)(2,1)} %t_hbm.1, bf16[64,12288]{1,0:T(8,128)(2,1)} %s_hbm.1, bf16[64,1000]{1,0:T(8,128)(2,1)} %w_hbm.1, s32[1,224]{1,0:T(1,128)} %bitcast.1, f32[64,768]{1,0:T(8,128)} %m1_hbm.1, f32[64,768]{1,0:T(8,128)} %m2_hbm.1), custom_call_target="tpu_custom_call" | custom-call | tf_op jit(solution)/shard_map/pallas_call | solution.py:529
  61.1 0.0 copy-start.1
  61.2 0.0 copy-start
  61.2 2.7 %copy.12 = bf16[64,12288]{1,0:T(8,128)(2,1)} copy(bf16[64,12288]{1,0:T(8,128)(2,1)} %get-tuple-element.6) | data formatting | bytes 3145728
  63.9 0.0 copy-done.1
  63.9 0.7 %copy.13 = f32[64,768]{1,0:T(8,128)} copy(f32[64,768]{1,0:T(8,128)S(1)} %copy-done.1) | data formatting | bytes 393216
  64.5 0.0 copy-done
  64.5 0.7 %copy.14 = f32[64,768]{1,0:T(8,128)} copy(f32[64,768]{1,0:T(8,128)S(1)} %copy-done) | data formatting | bytes 393216
Async XLA Ops:
  61.1 2.7 %copy-start.1 = (f32[64,768]{1,0:T(8,128)S(1)}, f32[64,768]{1,0:T(8,128)}, u32[]{:S(2)}) copy-start(f32[64,768]{1,0:T(8,128)} %get-tuple-element.7) | copy-start | bytes 589828
  61.2 3.4 %copy-start = (f32[64,768]{1,0:T(8,128)S(1)}, f32[64,768]{1,0:T(8,128)}, u32[]{:S(2)}) copy-start(f32[64,768]{1,0:T(8,128)} %get-tuple-element.8) | copy-start | bytes 589828

commit v3 on v2

--- a/solution.py
+++ b/solution.py
@@ -229,6 +229,17 @@
     barrier = pltpu.get_barrier_semaphore()
     for device in (SIB, YP, ZP, ZF, XP, AN):
         pl.semaphore_signal(barrier, inc=1, device_id=device, device_id_type=MESH)
+    load_s.wait()
+
+    def support_squares(i, acc):
+        block = sup_v[:, pl.ds(aligned(i * width, width), width)].astype(f32)
+        block = block * block
+        for k in range(width // 128):
+            acc = acc + block[:, k * 128 : (k + 1) * 128]
+        return acc
+
+    sacc = lax.fori_loop(0, pixels // width, support_squares, jnp.zeros((images, 128), f32))
+    s_row = to_row(jnp.sum(sacc, axis=1, keepdims=True), x * images, lanes)
     pl.semaphore_wait(barrier, 6)
 
     def piece(which, index):
@@ -245,39 +256,30 @@
         )
     send(w_hbm, lw.at[pl.ds(my_row, images), :], WEIGHTS, XP)
 
-    load_s.wait()
-
-    def support_squares(i, acc):
-        block = sup_v[:, pl.ds(aligned(i * width, width), width)].astype(f32)
-        block = block * block
-        for k in range(width // 128):
-            acc = acc + block[:, k * 128 : (k + 1) * 128]
-        return acc
-
-    sacc = lax.fori_loop(0, pixels // width, support_squares, jnp.zeros((images, 128), f32))
-    s_row = to_row(jnp.sum(sacc, axis=1, keepdims=True), x * images, lanes)
-    load_t.wait()
-    tacc[...] = jnp.zeros_like(tacc)
-
-    def target_squares(i, carry):
-        block = t_v[:, pl.ds(aligned(i * width, width), width)].astype(f32)
-        block = block * block
-        acc = tacc[...]
-        for k in range(width // 128):
-            acc = acc + block[:, k * 128 : (k + 1) * 128]
-        tacc[...] = acc
-        return carry
-
-    lax.fori_loop(0, half // width, target_squares, 0)
-    peer_first = aligned((1 - x) * mine_rows, mine_rows)
-    my_first = aligned(x * mine_rows, mine_rows)
-    peer_sq = jnp.sum(tacc[pl.ds(peer_first, mine_rows), :], axis=1, keepdims=True)
-    my_sq = jnp.sum(tacc[pl.ds(my_first, mine_rows), :], axis=1, keepdims=True)
-    load_l.wait()
-    label_col = to_col(labels_ref[...].astype(f32), mine_rows, x * mine_rows)
-    dmsg_s[0:8, :] = jnp.broadcast_to(to_row(peer_sq, 0, lanes), (8, lanes))
-    dmsg_s[8:16, :] = jnp.broadcast_to(s_row, (8, lanes))
-    send(dmsg_s, dmsg_r, DIAG, XP)
+    def target_sums():
+        load_t.wait()
+        tacc[...] = jnp.zeros_like(tacc)
+
+        def target_squares(i, carry):
+            block = t_v[:, pl.ds(aligned(i * width, width), width)].astype(f32)
+            block = block * block
+            acc = tacc[...]
+            for k in range(width // 128):
+                acc = acc + block[:, k * 128 : (k + 1) * 128]
+            tacc[...] = acc
+            return carry
+
+        lax.fori_loop(0, half // width, target_squares, 0)
+        peer_first = aligned((1 - x) * mine_rows, mine_rows)
+        my_first = aligned(x * mine_rows, mine_rows)
+        peer_sq = jnp.sum(tacc[pl.ds(peer_first, mine_rows), :], axis=1, keepdims=True)
+        my_sq = jnp.sum(tacc[pl.ds(my_first, mine_rows), :], axis=1, keepdims=True)
+        load_l.wait()
+        label_col = to_col(labels_ref[...].astype(f32), mine_rows, x * mine_rows)
+        dmsg_s[0:8, :] = jnp.broadcast_to(to_row(peer_sq, 0, lanes), (8, lanes))
+        dmsg_s[8:16, :] = jnp.broadcast_to(s_row, (8, lanes))
+        send(dmsg_s, dmsg_r, DIAG, XP)
+        return my_sq, my_first, peer_first, label_col
 
     load_o.wait()
     cacc[...] = jnp.zeros_like(cacc)
@@ -295,6 +297,8 @@
             send(here, here, SLAB + 2, YP)
             send(here, here, SLAB + 3, ZP)
         send(here, here, FWD + p, SIB)
+        if p == 0:
+            my_sq, my_first, peer_first, label_col = target_sums()
         cross_piece(piece(core, turn[p]))
         if p > 0:
             there = piece(1 - core, turn[p - 1])

time: 65.4 us -> 67 us (1.024); the launches traced: 65.2 us -> 65.9 us
  Pallas kernels: 60.5 us -> 61.2 us
    pallas_call x1, Pallas kernels: 60.5 us -> 61.2 us  [fused(): pl.pallas_call(functools.partial(step_kernel, scale, pixels), out_shape=(...]
where the time goes in v3:
time: 67 us; the launch traced here: 65.9 us
  Pallas kernels  61.2 us (91%)
  local copies, waits for them, and re-layouts  4.06 us (6%)
    pallas_call x1, Pallas kernels, fused(): pl.pallas_call(functools.partial(step_kernel, scale, pixels), out_shape=(...  61.2 us
    unnamed x7, local copies, waits for them, and re-layouts  4.06 us

profile of v3, /device:TPU:1, one launch (start us, length us, event | category | flops | bytes accessed | tf_op | source)
XLA Modules:
  0.0 65.9 jit_solution(18313795127030514186)
XLA Ops:
  0.6 61.2 %shard_map.85 = (bf16[64,12288]{1,0:T(8,128)(2,1)}, f32[64,768]{1,0:T(8,128)}, f32[64,768]{1,0:T(8,128)}) custom-call(bf16[224,6144]{1,0:T(8,128)(2,1)} %t_hbm.1, bf16[64,12288]{1,0:T(8,128)(2,1)} %s_hbm.1, bf16[64,1000]{1,0:T(8,128)(2,1)} %w_hbm.1, s32[1,224]{1,0:T(1,128)} %bitcast.1, f32[64,768]{1,0:T(8,128)} %m1_hbm.1, f32[64,768]{1,0:T(8,128)} %m2_hbm.1), custom_call_target="tpu_custom_call" | custom-call | tf_op jit(solution)/shard_map/pallas_call | solution.py:533
  61.8 0.0 copy-start.1
  61.8 0.0 copy-start
  61.8 2.7 %copy.12 = bf16[64,12288]{1,0:T(8,128)(2,1)} copy(bf16[64,12288]{1,0:T(8,128)(2,1)} %get-tuple-element.6) | data formatting | bytes 3145728
  64.5 0.0 copy-done.1
  64.5 0.7 %copy.13 = f32[64,768]{1,0:T(8,128)} copy(f32[64,768]{1,0:T(8,128)S(1)} %copy-done.1) | data formatting | bytes 393216
  65.2 0.0 copy-done
  65.2 0.7 %copy.14 = f32[64,768]{1,0:T(8,128)} copy(f32[64,768]{1,0:T(8,128)S(1)} %copy-done) | data formatting | bytes 393216
Async XLA Ops:
  61.8 2.7 %copy-start.1 = (f32[64,768]{1,0:T(8,128)S(1)}, f32[64,768]{1,0:T(8,128)}, u32[]{:S(2)}) copy-start(f32[64,768]{1,0:T(8,128)} %get-tuple-element.7) | copy-start | bytes 589828
  61.8 3.4 %copy-start = (f32[64,768]{1,0:T(8,128)S(1)}, f32[64,768]{1,0:T(8,128)}, u32[]{:S(2)}) copy-start(f32[64,768]{1,0:T(8,128)} %get-tuple-element.8) | copy-start | bytes 589828
